TPU v7x, 32 devices: a whole 2x2x4 slice. The times are simulated.
32 devices in a mesh: dp: 8 (over z, x), head: 4 (over y, core).
Axes of the slice: x: 2, y: 2, z: 4, core: 2. Of those that a mesh axis runs over, the one named last changes fastest.
Arguments:
- vit_ctx: bfloat16 [1024, 1536], P('dp', 'head'), may hold values from -6 to 6
- vit_resid: bfloat16 [1024, 1600], P('dp'), may hold values from -6 to 6
- vit_proj: bfloat16 [4, 384, 1600], P('head', 'dp'), may hold values from -0.15625 to 0.15625
- vit_grad: bfloat16 [1024, 1600], P('dp'), may hold values from -6 to 6
- norm_gain: float32 [1600], replicated, may hold values from 0.1 to 1.9
- cross_q: bfloat16 [96, 2048], P(None, 'head'), may hold values from -400 to 400
- key_w: bfloat16 [1600, 2048], P(None, 'head'), may hold values from -0.15625 to 0.15625
- value_w: bfloat16 [1600, 2048], P(None, 'head'), may hold values from -0.15625 to 0.15625
- out_w: bfloat16 [2048, 4096], P('head'), may hold values from -0.125 to 0.125
- query_state: bfloat16 [96, 4096], P(None, 'head'), may hold values from -1.5 to 1.5
Outputs:
- ctx_grad: bfloat16 [1024, 1536], P('dp', 'head')
- proj_grad: float32 [4, 384, 1600], P('head', 'dp')
- cross_out: bfloat16 [8, 96, 4096], P('dp', None, 'head')
All inputs are finite; a program needn't handle non-finite values.
Results may differ from a plain program's by a relative error of at most 0.017.
The roundings to bfloat16 on the way count: a program that leaves them out, or rounds other values in their place, can miss the bound.
Values may be sent and summed in bfloat16 or wider, within the bound.
A program may use at most 64 MiB of HBM per device.

v0:
```python
import math
import jax
import jax.numpy as jnp
from jax import lax
from jax.sharding import PartitionSpec as P

HD = 128
EPSILON = 1e-06


def on_device(
    vit_ctx, vit_resid, vit_proj, vit_grad, norm_gain, cross_q, key_w, value_w, out_w, query_state
):
    contract_cols = (((1,), (1,)), ((), ()))
    ctx_part = vit_ctx
    partial_value = jnp.dot(
        ctx_part,
        lax.all_gather(vit_proj, "dp", axis=1, tiled=True)[0],
        preferred_element_type=jnp.float32,
    )
    ctx_grad = lax.dot_general(
        vit_grad,
        lax.all_gather(vit_proj, "dp", axis=1, tiled=True)[0],
        contract_cols,
        preferred_element_type=jnp.float32,
    ).astype(jnp.bfloat16)
    ctx_part = vit_ctx
    grad_share = lax.psum_scatter(
        lax.dot_general(
            ctx_part, vit_grad, (((0,), (0,)), ((), ())), preferred_element_type=jnp.float32
        ),
        "dp",
        scatter_dimension=0,
        tiled=True,
    )
    proj_grad = grad_share[None]
    feature_count = partial_value.shape[1]
    summed = lax.psum(partial_value, "head")
    hidden = vit_resid.astype(jnp.float32) + summed
    row_mean = jnp.sum(hidden, axis=1, keepdims=True) / feature_count
    square_mean = jnp.sum(hidden * hidden, axis=1, keepdims=True) / feature_count
    variance = square_mean - row_mean * row_mean
    features = ((hidden - row_mean) * lax.rsqrt(variance + EPSILON) * norm_gain).astype(
        jnp.bfloat16
    )
    head_count = key_w.shape[1] // HD
    query_count = cross_q.shape[0]
    key_rows = jnp.dot(features, key_w, preferred_element_type=jnp.float32).astype(jnp.bfloat16)
    value_rows = jnp.dot(features, value_w, preferred_element_type=jnp.float32).astype(jnp.bfloat16)
    queries = cross_q.reshape(query_count, head_count, HD)
    key_heads = key_rows.reshape(-1, head_count, HD)
    value_heads = value_rows.reshape(-1, head_count, HD)
    score_scale = 1.0 / math.sqrt(HD)
    scores = (
        jnp.einsum("qhd,khd->hqk", queries, key_heads, preferred_element_type=jnp.float32)
        * score_scale
    )
    row_max = jnp.max(scores, axis=2, keepdims=True)
    exponent = jnp.exp(scores - row_max)
    attn_probs = (exponent / jnp.sum(exponent, axis=2, keepdims=True)).astype(jnp.bfloat16)
    attended = jnp.einsum(
        "hqk,khd->qhd", attn_probs, value_heads, preferred_element_type=jnp.float32
    )
    attended = attended.astype(jnp.bfloat16).reshape(query_count, head_count * HD)
    out_partial = jnp.dot(attended, out_w, preferred_element_type=jnp.float32)
    out_share = lax.psum_scatter(
        out_partial.astype(jnp.bfloat16), "head", scatter_dimension=1, tiled=True
    ).astype(jnp.float32)
    cross_out = (out_share + query_state.astype(jnp.float32)).astype(jnp.bfloat16)[None]
    return (ctx_grad, proj_grad, cross_out)


def solution(mesh):
    return jax.shard_map(
        on_device,
        mesh=mesh,
        in_specs=(
            P("dp", "head"),
            P("dp", None),
            P("head", "dp", None),
            P("dp", None),
            P(),
            P(None, "head"),
            P(None, "head"),
            P(None, "head"),
            P("head", None),
            P(None, "head"),
        ),
        out_specs=(P("dp", "head"), P("head", "dp", None), P("dp", None, "head")),
        check_vma=False,
    )
```

profile of v0, /device:TPU:0, one launch (start us, length us, event | category | flops | bytes accessed | tf_op | source)
XLA Modules:
  0.0 205.2 jit_solution(9115707101834075549)
XLA Ops:
  7.2 0.0 copy-start
  7.2 0.0 all-gather.2.cloned.1.call-start
  7.2 0.7 all-gather.2.cloned.1.call-update
  7.9 0.0 copy-start.9
  7.9 0.0 all-reduce.2.cloned.1.call-start
  8.0 46.6 %all-gather.2.cloned.1.call-done = bf16[1,384,1600]{2,1,0:T(8,128)(2,1)} async-done(((bf16[1,48,1600]{2,1,0:T(8,128)(2,1)}), bf16[1,384,1600]{2,1,0:T(8,128)(2,1)}) %all-gather.2.cloned.1.call-update) | async-done | bytes 1228816 | tf_op jit(solution)/shard_map/all_gather | solution.py:23
  54.6 2.9 %fusion.1 = f32[128,1600]{0,1:T(8,128)} fusion(bf16[128,384]{1,0:T(8,128)(2,1)} %param.10, bf16[1,384,1600]{2,1,0:T(8,128)(2,1)} %all-gather.2.cloned.1.call-done), kind=kOutput, calls=%fused_computation.2 | convolution fusion | flops 157286400 | bytes 2146304 | tf_op jit(solution)/shard_map/dot_general | solution.py:16
  57.5 0.0 all-reduce.2.cloned.1.call-update
  57.5 0.0 reduce-scatter.5.cloned.1.call-start
  57.6 34.2 %all-reduce.2.cloned.1.call-done = f32[128,1600]{0,1:T(8,128)} async-done(((f32[128,1600]{0,1:T(8,128)}), f32[128,1600]{0,1:T(8,128)}) %all-reduce.2.cloned.1.call-update) | async-done | bytes 819216 | tf_op jit(solution)/shard_map/psum | solution.py:38
  91.8 0.0 copy-done.5
  91.8 1.4 fusion.14
  93.3 0.0 copy-start.4
  93.3 0.3 multiply_convert_fusion
  93.6 0.0 copy-start.8
  93.6 0.4 fusion.12
  94.1 0.7 copy-done.4
  94.7 0.4 fusion.11
  95.2 0.2 fusion.6
  95.4 0.2 fusion.26
  95.6 0.7 fusion.13
  96.4 0.0 copy-start.6
  96.4 3.9 %convolution_convert_fusion = bf16[96,4096]{1,0:T(8,128)(2,1)} fusion(bf16[512,4096]{1,0:T(8,128)(2,1)} %param.18, bf16[4,12,8,128]{3,2,1,0:T(8,128)(2,1)S(1)} %fusion.13), kind=kOutput, calls=%fused_computation.1 | convolution fusion | flops 403046400 | bytes 5079040 | tf_op jit(solution)/shard_map/dot_general | solution.py:65
  100.3 0.0 reduce-scatter.5.cloned.1.call-update
  100.3 0.0 reduce-scatter.3.cloned.1.call-start
  100.4 2.0 fusion.27
  102.4 0.0 reduce-scatter.3.cloned.1.call-update
  102.4 1.3 copy-done.1
  103.7 1.2 fusion.8
  104.8 18.8 %reduce-scatter.5.cloned.1.call-done = bf16[96,1024]{1,0:T(8,128)(2,1)} async-done(((bf16[96,4096]{1,0:T(8,128)(2,1)}), bf16[96,1024]{1,0:T(8,128)(2,1)}) %reduce-scatter.5.cloned.1.call-update) | async-done | bytes 196624 | tf_op jit(solution)/shard_map/reduce_scatter | solution.py:66
  123.7 1.7 fusion.15
  125.3 73.4 %reduce-scatter.3.cloned.1.call-done = f32[48,1600]{1,0:T(8,128)} async-done(((f32[384,1600]{1,0:T(8,128)}), f32[48,1600]{1,0:T(8,128)}) %reduce-scatter.3.cloned.1.call-update) | async-done | bytes 307216 | tf_op jit(solution)/shard_map/reduce_scatter | solution.py:28
  (13 shorter events, 0.0 us)
Async XLA Ops:
  7.2 86.4 %copy-start = (bf16[1600,512]{1,0:T(8,128)(2,1)S(1)}, bf16[1600,512]{1,0:T(8,128)(2,1)}, u32[]{:S(2)}) copy-start(bf16[1600,512]{1,0:T(8,128)(2,1)} %param.16) | copy-start | bytes 4915204
  7.2 84.6 %copy-start.5 = (bf16[128,1600]{0,1:T(8,128)(2,1)S(1)}, bf16[128,1600]{0,1:T(8,128)(2,1)}, u32[]{:S(2)}) copy-start(bf16[128,1600]{0,1:T(8,128)(2,1)} %param.11) | copy-start | bytes 1228804
  7.2 47.4 %all-gather.2.cloned.1.call-start = ((), (), s32[]{:S(2)}) async-start(), calls=%async_computation.2 | async-start | bytes 1437696 | tf_op jit(solution)/shard_map/all_gather | solution.py:23
  7.9 85.3 %copy-start.9 = (f32[1600]{0:T(1024)S(1)}, f32[1600]{0:T(1024)}, u32[]{:S(2)}) copy-start(f32[1600]{0:T(1024)} %param.14) | copy-start | bytes 19204
  7.9 83.9 %all-reduce.2.cloned.1.call-start = ((), (), s32[]{:S(2)}) async-start(), calls=%async_computation.4 | async-start | bytes 1638400 | tf_op jit(solution)/shard_map/psum | solution.py:38
  57.5 66.1 %reduce-scatter.5.cloned.1.call-start = ((), (), s32[]{:S(2)}) async-start(), calls=%async_computation.5 | async-start | bytes 983040 | tf_op jit(solution)/shard_map/reduce_scatter | solution.py:66
  91.8 1.5 copy-start.2
  93.3 1.4 copy-start.4
  93.6 1.6 copy-start.8
  96.4 4.0 %copy-start.3 = (bf16[128,1600]{0,1:T(8,128)(2,1)S(1)}, bf16[128,1600]{0,1:T(8,128)(2,1)}, u32[]{:S(2)}) copy-start(bf16[128,1600]{0,1:T(8,128)(2,1)} %param.13) | copy-start | bytes 1228804
  96.4 4.0 %copy-start.6 = (bf16[128,384]{1,0:T(8,128)(2,1)S(1)}, bf16[128,384]{1,0:T(8,128)(2,1)}, u32[]{:S(2)}) copy-start(bf16[128,384]{1,0:T(8,128)(2,1)} %param.10) | copy-start | bytes 294916
  100.3 98.4 %reduce-scatter.3.cloned.1.call-start = ((), (), s32[]{:S(2)}) async-start(), calls=%async_computation.3 | async-start | bytes 2875392 | tf_op jit(solution)/shard_map/reduce_scatter | solution.py:28
  102.4 1.3 copy-start.1
  102.4 21.3 %copy-start.7 = (bf16[96,1024]{1,0:T(8,128)(2,1)S(1)}, bf16[96,1024]{1,0:T(8,128)(2,1)}, u32[]{:S(2)}) copy-start(bf16[96,1024]{1,0:T(8,128)(2,1)} %param.19) | copy-start | bytes 589828
Sparse Core Ops, SparseCore 0:
  10.2 44.4 all-gather.1
  57.7 34.0 all-reduce.1
  100.4 23.1 reduce-scatter.4
  127.6 71.0 reduce-scatter.2
where the time goes:
time: 205 us
  waiting for transfers between devices  174 us (85%)
  between operations  13.9 us (7%)
  matrix products  11.8 us (6%)
  other arithmetic  3.64 us (2%)
    reduce_scatter x1, waiting for transfers between devices, on_device(): lax.psum_scatter(lax.dot_general(ctx_part, vit_grad, (((0,), (0,)), ((),...  73.4 us
    all_gather x1, waiting for transfers between devices, on_device(): lax.all_gather(vit_proj, 'dp', axis=1, tiled=True)[0]  46.6 us
    psum x1, waiting for transfers between devices, on_device(): summed = lax.psum(partial_value, 'head')  34.2 us
    reduce_scatter x1, waiting for transfers between devices, on_device(): lax.psum_scatter(out_partial.astype(jnp.bfloat16), 'head', scatter_dimens...  18.8 us
  transfers between devices with their start and end apart: 4, of which 4 were waited for; matrix products, arithmetic and copies ran while one was open for 2% of the time, Pallas kernels for 0%

commit v1 on v0

--- a/solution.py
+++ b/solution.py
@@ -35,7 +35,9 @@
     )
     proj_grad = grad_share[None]
     feature_count = partial_value.shape[1]
-    summed = lax.psum(partial_value, "head")
+    summed = partial_value
+    for hop in (1, 2):
+        summed = summed + lax.ppermute(summed, "head", [(dev, dev ^ hop) for dev in range(4)])
     hidden = vit_resid.astype(jnp.float32) + summed
     row_mean = jnp.sum(hidden, axis=1, keepdims=True) / feature_count
     square_mean = jnp.sum(hidden * hidden, axis=1, keepdims=True) / feature_count

time: 205 us -> 191 us (0.932)
  waiting for transfers between devices: 174 us -> 160 us
    psum x1 -> x0, waiting for transfers between devices: 34.2 us -> none  [on_device(): summed = lax.psum(partial_value, 'head')]
    ppermute x0 -> x2, waiting for transfers between devices: none -> 21.1 us  [on_device(): lax.ppermute(summed, 'head', [(dev, dev ^ hop) for dev in range(4)])]
  transfers between devices with their start and end apart: 4 -> 5, of which waited for: 4 -> 5; matrix products, arithmetic and copies ran while one was open for 2% -> 3% of each run, Pallas kernels for 0% -> 0%
where the time goes in v1:
time: 191 us
  waiting for transfers between devices  160 us (84%)
  between operations  13.9 us (7%)
  matrix products  11.8 us (6%)
  other arithmetic  2.22 us (1%)
    reduce_scatter x1, waiting for transfers between devices, on_device(): lax.psum_scatter(lax.dot_general(ctx_part, vit_grad, (((0,), (0,)), ((),...  73.4 us
    all_gather x1, waiting for transfers between devices, on_device(): lax.all_gather(vit_proj, 'dp', axis=1, tiled=True)[0]  46.6 us
    ppermute x2, waiting for transfers between devices, on_device(): lax.ppermute(summed, 'head', [(dev, dev ^ hop) for dev in range(4)])  21.1 us
    reduce_scatter x1, waiting for transfers between devices, on_device(): lax.psum_scatter(out_partial.astype(jnp.bfloat16), 'head', scatter_dimens...  17.7 us
    dot_general x1, matrix products, on_device(): out_partial = jnp.dot(attended, out_w, preferred_element_type=jnp.float32)  3.92 us
  transfers between devices with their start and end apart: 5, of which 5 were waited for; matrix products, arithmetic and copies ran while one was open for 3% of the time, Pallas kernels for 0%

profile of v1, /device:TPU:0, one launch (start us, length us, event | category | flops | bytes accessed | tf_op | source)
XLA Modules:
  0.0 191.0 jit_solution(8808292167261373039)
XLA Ops:
  7.2 0.0 copy-start
  7.2 0.0 all-gather.2.cloned.1.call-start
  7.2 0.7 all-gather.2.cloned.1.call-update
  7.9 0.0 reduce-scatter.5.cloned.1.call-start
  8.0 46.6 %all-gather.2.cloned.1.call-done = bf16[1,384,1600]{2,1,0:T(8,128)(2,1)} async-done(((bf16[1,48,1600]{2,1,0:T(8,128)(2,1)}), bf16[1,384,1600]{2,1,0:T(8,128)(2,1)}) %all-gather.2.cloned.1.call-update) | async-done | bytes 1228816 | tf_op jit(solution)/shard_map/all_gather | solution.py:23
  54.6 2.0 %fusion.1 = f32[128,1600]{0,1:T(8,128)S(1)} fusion(bf16[128,384]{1,0:T(8,128)(2,1)} %param.10, bf16[1,384,1600]{2,1,0:T(8,128)(2,1)} %all-gather.2.cloned.1.call-done), kind=kOutput, calls=%fused_computation.2 | convolution fusion | flops 157286400 | bytes 2146304 | tf_op jit(solution)/shard_map/dot_general | solution.py:16
  56.6 0.0 copy-start.4
  56.6 0.1 collective-permute-start
  56.7 2.3 %collective-permute-done = f32[128,1600]{0,1:T(8,128)S(1)} collective-permute-done((f32[128,1600]{0,1:T(8,128)S(1)}, f32[128,1600]{0,1:T(8,128)S(1)}, u32[]{:S(2)}, u32[]{:S(2)}) %collective-permute-start) | collective-permute-done | bytes 819232 | tf_op jit(solution)/shard_map/ppermute | solution.py:40
  59.0 0.1 add.27
  59.1 0.0 copy-start.8
  59.1 1.5 collective-permute-start.1
  60.7 18.8 %collective-permute-done.1 = f32[128,1600]{0,1:T(8,128)S(1)} collective-permute-done((f32[128,1600]{0,1:T(8,128)S(1)}, f32[128,1600]{0,1:T(8,128)S(1)}, u32[]{:S(2)}, u32[]{:S(2)}) %collective-permute-start.1) | collective-permute-done | bytes 819232 | tf_op jit(solution)/shard_map/ppermute | solution.py:40
  79.5 0.2 fusion.25
  79.7 0.0 copy-start.3
  79.7 0.9 fusion.12
  80.7 0.5 copy-done.3
  81.1 0.9 fusion.11
  82.1 0.2 fusion.6
  82.3 0.2 fusion.26
  82.5 0.7 fusion.13
  83.2 0.0 copy-start.5
  83.3 3.9 %convolution_convert_fusion = bf16[96,4096]{1,0:T(8,128)(2,1)} fusion(bf16[512,4096]{1,0:T(8,128)(2,1)} %param.18, bf16[4,12,8,128]{3,2,1,0:T(8,128)(2,1)S(1)} %fusion.13), kind=kOutput, calls=%fused_computation.1 | convolution fusion | flops 403046400 | bytes 5079040 | tf_op jit(solution)/shard_map/dot_general | solution.py:67
  87.2 0.0 reduce-scatter.5.cloned.1.call-update
  87.2 0.0 reduce-scatter.3.cloned.1.call-start
  87.3 2.0 %fusion.27 = f32[384,1600]{1,0:T(8,128)} fusion(bf16[128,384]{1,0:T(8,128)(2,1)S(1)} %copy-done.5, bf16[128,1600]{0,1:T(8,128)(2,1)S(1)} %copy-done.2), kind=kOutput, calls=%fused_computation.37 | convolution fusion | flops 157286400 | bytes 2965504 | tf_op jit(solution)/shard_map/dot_general | solution.py:29
  89.3 0.0 reduce-scatter.3.cloned.1.call-update
  89.3 1.3 copy-done.1
  90.6 1.2 fusion.8
  91.7 17.7 %reduce-scatter.5.cloned.1.call-done = bf16[96,1024]{1,0:T(8,128)(2,1)} async-done(((bf16[96,4096]{1,0:T(8,128)(2,1)}), bf16[96,1024]{1,0:T(8,128)(2,1)}) %reduce-scatter.5.cloned.1.call-update) | async-done | bytes 196624 | tf_op jit(solution)/shard_map/reduce_scatter | solution.py:68
  109.4 1.7 fusion.14
  111.1 73.4 %reduce-scatter.3.cloned.1.call-done = f32[48,1600]{1,0:T(8,128)} async-done(((f32[384,1600]{1,0:T(8,128)}), f32[48,1600]{1,0:T(8,128)}) %reduce-scatter.3.cloned.1.call-update) | async-done | bytes 307216 | tf_op jit(solution)/shard_map/reduce_scatter | solution.py:28
  (12 shorter events, 0.0 us)
Async XLA Ops:
  7.2 72.6 %copy-start = (bf16[1600,512]{1,0:T(8,128)(2,1)S(1)}, bf16[1600,512]{1,0:T(8,128)(2,1)}, u32[]{:S(2)}) copy-start(bf16[1600,512]{1,0:T(8,128)(2,1)} %param.16) | copy-start | bytes 4915204
  7.2 47.4 %all-gather.2.cloned.1.call-start = ((), (), s32[]{:S(2)}) async-start(), calls=%async_computation.2 | async-start | bytes 1437696 | tf_op jit(solution)/shard_map/all_gather | solution.py:23
  7.9 101.5 %reduce-scatter.5.cloned.1.call-start = ((), (), s32[]{:S(2)}) async-start(), calls=%async_computation.4 | async-start | bytes 983040 | tf_op jit(solution)/shard_map/reduce_scatter | solution.py:68
  56.6 22.9 %copy-start.4 = (bf16[128,1600]{0,1:T(8,128)(2,1)S(1)}, bf16[128,1600]{0,1:T(8,128)(2,1)}, u32[]{:S(2)}) copy-start(bf16[128,1600]{0,1:T(8,128)(2,1)} %param.11) | copy-start | bytes 1228804
  56.6 2.4 %collective-permute-start = (f32[128,1600]{0,1:T(8,128)S(1)}, f32[128,1600]{0,1:T(8,128)S(1)}, u32[]{:S(2)}, u32[]{:S(2)}) collective-permute-start(f32[128,1600]{0,1:T(8,128)S(1)} %fusion.1), channel_id=1, source_target_pairs={{0,1},{1,0},{2,3},{3,2},{4,5},{5,4},{6,7},{7,6},{8,9},{9,8},{10,11... | collective-permute-start | bytes 2457608 | tf_op jit(solution)/shard_map/ppermute | solution.py:40
  59.1 20.6 %copy-start.8 = (f32[1600]{0:T(1024)S(1)}, f32[1600]{0:T(1024)}, u32[]{:S(2)}) copy-start(f32[1600]{0:T(1024)} %param.14) | copy-start | bytes 19204
  59.1 20.4 %collective-permute-start.1 = (f32[128,1600]{0,1:T(8,128)S(1)}, f32[128,1600]{0,1:T(8,128)S(1)}, u32[]{:S(2)}, u32[]{:S(2)}) collective-permute-start(f32[128,1600]{0,1:T(8,128)S(1)} %add.27), channel_id=1, source_target_pairs={{0,2},{1,3},{2,0},{3,1},{4,6},{5,7},{6,4},{7,5},{8,10},{9,11},{10,... | collective-permute-start | bytes 2457608 | tf_op jit(solution)/shard_map/ppermute | solution.py:40
  79.7 1.4 copy-start.3
  81.1 0.9 copy-start.7
  83.2 4.0 %copy-start.2 = (bf16[128,1600]{0,1:T(8,128)(2,1)S(1)}, bf16[128,1600]{0,1:T(8,128)(2,1)}, u32[]{:S(2)}) copy-start(bf16[128,1600]{0,1:T(8,128)(2,1)} %param.13) | copy-start | bytes 1228804
  83.2 4.0 %copy-start.5 = (bf16[128,384]{1,0:T(8,128)(2,1)S(1)}, bf16[128,384]{1,0:T(8,128)(2,1)}, u32[]{:S(2)}) copy-start(bf16[128,384]{1,0:T(8,128)(2,1)} %param.10) | copy-start | bytes 294916
  87.2 97.2 %reduce-scatter.3.cloned.1.call-start = ((), (), s32[]{:S(2)}) async-start(), calls=%async_computation.3 | async-start | bytes 2875392 | tf_op jit(solution)/shard_map/reduce_scatter | solution.py:28
  89.3 1.3 copy-start.1
  89.3 20.1 %copy-start.6 = (bf16[96,1024]{1,0:T(8,128)(2,1)S(1)}, bf16[96,1024]{1,0:T(8,128)(2,1)}, u32[]{:S(2)}) copy-start(bf16[96,1024]{1,0:T(8,128)(2,1)} %param.19) | copy-start | bytes 589828
Sparse Core Ops, SparseCore 0:
  10.2 44.4 all-gather.1
  87.3 22.0 reduce-scatter.4
  113.5 70.8 reduce-scatter.2
